TPU v7x, 32 devices: a whole 2x2x4 slice. The times are simulated.
32 devices in a mesh: dp: 8 (over z, y), tensor: 4 (over x, core).
Axes of the slice: x: 2, y: 2, z: 4, core: 2. Of those that a mesh axis runs over, the one named last changes fastest.
Arguments:
- inputs: bfloat16 [4096, 768], P(('dp', 'tensor')), may hold values from -6 to 6
- prev_logits: bfloat16 [4096, 12, 4096], P('dp', 'tensor'), may hold values from -6 to 6
- w_query: bfloat16 [768, 768], P('dp', 'tensor'), may hold values from -0.21875 to 0.21875
- w_key: bfloat16 [768, 768], P('dp', 'tensor'), may hold values from -0.21875 to 0.21875
- w_value: bfloat16 [768, 768], P('dp', 'tensor'), may hold values from -0.21875 to 0.21875
- w_attn_out: bfloat16 [768, 768], P('tensor', 'dp'), may hold values from -2.5 to 2.5
- w_ffn_in: bfloat16 [768, 3072], P('dp', 'tensor'), may hold values from -0.21875 to 0.21875
- ffn_bias: bfloat16 [3072], P(('tensor', 'dp')), may hold values from -3 to 3
- w_ffn_out: bfloat16 [3072, 768], P(('tensor', 'dp')), may hold values from -0.109375 to 0.109375
- norm1_gain: float32 [768], replicated, may hold values from 0.5 to 1.5
- norm1_shift: float32 [768], replicated, may hold values from -2 to 2
- norm2_gain: float32 [768], replicated, may hold values from 0.5 to 1.5
- norm2_shift: float32 [768], replicated, may hold values from -2 to 2
- token_segment: int32 [4096], replicated, may hold values from 0 to 12, as said below
- segment_parent: int32 [1, 13], replicated, may hold values from 0 to 4, as said below
- out_grad: bfloat16 [4096, 768], P(('dp', 'tensor')), may hold values from -6 to 6
- logit_grad: bfloat16 [4096, 12, 4096], P('dp', 'tensor'), may hold values from -6 to 6
Outputs:
- output: bfloat16 [4096, 768], P(('dp', 'tensor'))
- logits: bfloat16 [4096, 12, 4096], P('dp', 'tensor')
- input_grad: float32 [4096, 768], P(('dp', 'tensor'))
- prev_grad: bfloat16 [4096, 12, 4096], P('dp', 'tensor')
- w_query_grad: float32 [768, 768], P('dp', 'tensor')
- w_key_grad: float32 [768, 768], P('dp', 'tensor')
- w_value_grad: float32 [768, 768], P('dp', 'tensor')
- w_attn_out_grad: float32 [768, 768], P('tensor', 'dp')
- w_ffn_in_grad: float32 [768, 3072], P('dp', 'tensor')
- ffn_bias_grad: float32 [3072], P(('tensor', 'dp'))
- w_ffn_out_grad: float32 [3072, 768], P(('tensor', 'dp'))
- norm1_gain_grad: float32 [768], replicated
- norm1_shift_grad: float32 [768], replicated
- norm2_gain_grad: float32 [768], replicated
- norm2_shift_grad: float32 [768], replicated
Inputs may be any that keep to these rules, and one draw needn't show every extreme that they name: `token_segment`: in each tree the first 2048 tokens are segment 0, the trunk; the other tokens hold the 4 branches (segments 1 to 4, 256 tokens each) and the 8 leaves (segments 5 to 12, 128 tokens each), each segment one contiguous run, in an order that varies from tree to tree. `segment_parent`: row t lists the parents of tree t's segments: 0 for the trunk and every branch, a branch for every leaf, each branch the parent of exactly two leaves.
All inputs are finite; a program needn't handle non-finite values.
Results may differ from a plain program's by a relative error of at most 0.017.
Values may be sent and summed in bfloat16 or wider, within the bound.
No kernel may reach another device: no remote copies, remote signals or barrier semaphores. Data moves between devices by JAX's collectives and lax.ppermute only.
A program may use at most 256 MiB of HBM per device.

v0:
```python
import jax
import jax.numpy as jnp
from jax import lax
from jax.sharding import PartitionSpec as P

E = 64


EPSILON = 1e-12


def layer_norm(values, norm_gain, norm_shift):
    center = values - jnp.mean(values, axis=-1, keepdims=True)
    spread = jnp.mean(center * center, axis=-1, keepdims=True)
    return center * lax.rsqrt(spread + EPSILON) * norm_gain + norm_shift


def gelu_exact(values):
    return jax.nn.gelu(values, approximate=False)


def attend_forward(key_count, local_heads, head_dim, score_scale):
    columns = local_heads * head_dim

    def run(operands):
        query_heads, tree_kv, previous, allowed = operands
        group_rows = query_heads.shape[0]
        key_heads = tree_kv[:key_count, :columns].reshape(key_count, local_heads, head_dim)
        value_heads = tree_kv[:key_count, columns:].reshape(key_count, local_heads, head_dim)
        scores = jnp.einsum(
            "qhe,khe->qhk", query_heads, key_heads, preferred_element_type=jnp.float32
        ) * score_scale + previous.astype(jnp.float32)
        logits = jnp.where(allowed, scores, 0.0).astype(jnp.bfloat16)
        masked = jnp.where(allowed, scores, -jnp.inf)
        row_max = jnp.max(masked, axis=-1, keepdims=True)
        exponent = jnp.exp(masked - row_max)
        row_total = jnp.sum(exponent, axis=-1, keepdims=True)
        log_total = row_max + jnp.log(row_total)
        weights = (exponent / row_total).astype(jnp.bfloat16)
        mixed = (
            jnp.einsum("qhk,khe->qhe", weights, value_heads, preferred_element_type=jnp.float32)
            .astype(jnp.bfloat16)
            .reshape(group_rows, columns)
        )
        return (mixed, logits, log_total)

    return run


def attend_backward(key_count, local_heads, head_dim, score_scale):
    columns = local_heads * head_dim

    def run(operands):
        query_heads, tree_kv, previous, allowed, log_total, grad_mixed_heads, upstream = operands
        group_rows = query_heads.shape[0]
        key_heads = tree_kv[:key_count, :columns].reshape(key_count, local_heads, head_dim)
        value_heads = tree_kv[:key_count, columns:].reshape(key_count, local_heads, head_dim)
        scores = jnp.einsum(
            "qhe,khe->qhk", query_heads, key_heads, preferred_element_type=jnp.float32
        ) * score_scale + previous.astype(jnp.float32)
        attention_weight = jnp.exp(jnp.where(allowed, scores, -jnp.inf) - log_total)
        grad_weight = jnp.einsum(
            "qhe,khe->qhk", grad_mixed_heads, value_heads, preferred_element_type=jnp.float32
        )
        grad_values = jnp.einsum(
            "qhk,qhe->khe",
            attention_weight.astype(jnp.bfloat16),
            grad_mixed_heads,
            preferred_element_type=jnp.float32,
        )
        grad_soft = attention_weight * (
            grad_weight - jnp.sum(attention_weight * grad_weight, axis=-1, keepdims=True)
        )
        grad_scores = jnp.where(allowed, upstream.astype(jnp.float32) + grad_soft, 0.0).astype(
            jnp.bfloat16
        )
        grad_query = (
            (
                jnp.einsum(
                    "qhk,khe->qhe", grad_scores, key_heads, preferred_element_type=jnp.float32
                )
                * score_scale
            )
            .astype(jnp.bfloat16)
            .reshape(group_rows, columns)
        )
        grad_keys = (
            jnp.einsum("qhk,qhe->khe", grad_scores, query_heads, preferred_element_type=jnp.float32)
            * score_scale
        )
        tree_grads = jnp.concatenate(
            [grad_keys.reshape(key_count, columns), grad_values.reshape(key_count, columns)], axis=1
        )
        return (grad_scores, grad_query, tree_grads)

    return run


def shards(
    inputs,
    prev_logits,
    w_query,
    w_key,
    w_value,
    w_attn_out,
    w_ffn_in,
    ffn_bias,
    w_ffn_out,
    norm1_gain,
    norm1_shift,
    norm2_gain,
    norm2_shift,
    token_segment,
    segment_parent,
    out_grad,
    logit_grad,
):
    group_rows = prev_logits.shape[0]
    local_heads = prev_logits.shape[1]
    tree_len = prev_logits.shape[2]
    head_dim = E
    columns = local_heads * head_dim
    spread = tree_len // group_rows
    score_scale = head_dim ** (-0.5)
    data_index = lax.axis_index("dp")
    tree_index = data_index // spread
    local_index = data_index % spread
    query_start = local_index * group_rows
    full_query, full_key, full_value, full_attn, full_inner, full_bias, full_outer = (
        lax.all_gather(w_query, "dp", axis=0, tiled=True),
        lax.all_gather(w_key, "dp", axis=0, tiled=True),
        lax.all_gather(w_value, "dp", axis=0, tiled=True),
        lax.all_gather(w_attn_out, "dp", axis=1, tiled=True),
        lax.all_gather(w_ffn_in, "dp", axis=0, tiled=True),
        lax.all_gather(ffn_bias, "dp", axis=0, tiled=True),
        lax.all_gather(w_ffn_out, "dp", axis=0, tiled=True),
    )
    full_project = jnp.concatenate([full_query, full_key, full_value], axis=1)
    rows_all = lax.all_gather(inputs, "tensor", axis=0, tiled=True)
    projected = jnp.dot(rows_all, full_project, preferred_element_type=jnp.float32).astype(
        jnp.bfloat16
    )
    query = projected[:, :columns]
    kv_local = projected[:, columns:]
    everything = lax.all_gather(kv_local, "dp", axis=0, tiled=True)
    tree_kv = lax.dynamic_slice_in_dim(everything, tree_index * tree_len, tree_len, 0)
    seg_tree = lax.dynamic_slice_in_dim(token_segment, tree_index * tree_len, tree_len, 0)
    seg_rows = lax.dynamic_slice_in_dim(seg_tree, query_start, group_rows, 0)
    parents = lax.dynamic_slice_in_dim(segment_parent, tree_index, 1, 0)[0]
    labels = jnp.arange(parents.shape[0], dtype=jnp.int32)
    parent_one = jnp.sum(
        jnp.where(seg_rows[:, None] == labels[None, :], parents[None, :], 0), axis=1
    )
    parent_two = jnp.sum(
        jnp.where(parent_one[:, None] == labels[None, :], parents[None, :], 0), axis=1
    )
    allowed = (
        (seg_tree[None, :] == seg_rows[:, None])
        | (seg_tree[None, :] == parent_one[:, None])
        | (seg_tree[None, :] == parent_two[:, None])
    )[:, None, :]
    query_heads = query.reshape(group_rows, local_heads, head_dim)
    forward_all = attend_forward(tree_len, local_heads, head_dim, score_scale)
    forward_operands = (query_heads, tree_kv, prev_logits, allowed)
    mixed, logits, log_total = forward_all(forward_operands)
    attended = lax.psum_scatter(
        jnp.dot(mixed, full_attn, preferred_element_type=jnp.float32).astype(jnp.bfloat16),
        "tensor",
        scatter_dimension=0,
        tiled=True,
    ).astype(jnp.float32)
    first_sum = inputs.astype(jnp.float32) + attended
    hidden, norm_one_back = jax.vjp(layer_norm, first_sum, norm1_gain, norm1_shift)
    hidden_all = lax.all_gather(hidden.astype(jnp.bfloat16), "tensor", axis=0, tiled=True)
    inner_raw = jnp.dot(
        hidden_all, full_inner, preferred_element_type=jnp.float32
    ) + full_bias.astype(jnp.float32)
    active, gelu_back = jax.vjp(gelu_exact, inner_raw)
    active_low = active.astype(jnp.bfloat16)
    ffn_out = lax.psum_scatter(
        jnp.dot(active_low, full_outer, preferred_element_type=jnp.float32).astype(jnp.bfloat16),
        "tensor",
        scatter_dimension=0,
        tiled=True,
    ).astype(jnp.float32)
    result, norm_two_back = jax.vjp(layer_norm, hidden + ffn_out, norm2_gain, norm2_shift)
    grad_second, grad_gain_two, grad_shift_two = norm_two_back(out_grad.astype(jnp.float32))
    grad_rows_all = lax.all_gather(grad_second.astype(jnp.bfloat16), "tensor", axis=0, tiled=True)
    grad_active = jnp.dot(grad_rows_all, full_outer.T, preferred_element_type=jnp.float32).astype(
        jnp.bfloat16
    )
    grad_w_outer = jnp.dot(active_low.T, grad_rows_all, preferred_element_type=jnp.float32)
    (grad_inner,) = gelu_back(grad_active.astype(jnp.float32))
    grad_inner_low = grad_inner.astype(jnp.bfloat16)
    grad_bias = jnp.sum(grad_inner_low.astype(jnp.float32), axis=0)
    grad_w_inner = jnp.dot(hidden_all.T, grad_inner_low, preferred_element_type=jnp.float32)
    grad_hidden = grad_second + lax.psum_scatter(
        jnp.dot(grad_inner_low, full_inner.T, preferred_element_type=jnp.float32).astype(
            jnp.bfloat16
        ),
        "tensor",
        scatter_dimension=0,
        tiled=True,
    ).astype(jnp.float32)
    grad_first, grad_gain_one, grad_shift_one = norm_one_back(grad_hidden)
    grad_attn_all = lax.all_gather(grad_first.astype(jnp.bfloat16), "tensor", axis=0, tiled=True)
    grad_mixed = jnp.dot(grad_attn_all, full_attn.T, preferred_element_type=jnp.float32).astype(
        jnp.bfloat16
    )
    grad_w_attn = jnp.dot(mixed.T, grad_attn_all, preferred_element_type=jnp.float32)
    grad_mixed_heads = grad_mixed.reshape(group_rows, local_heads, head_dim)
    backward_all = attend_backward(tree_len, local_heads, head_dim, score_scale)
    backward_operands = (
        query_heads,
        tree_kv,
        prev_logits,
        allowed,
        log_total,
        grad_mixed_heads,
        logit_grad,
    )
    grad_scores, grad_query, tree_grads = backward_all(backward_operands)
    placed = lax.dynamic_update_slice_in_dim(
        jnp.zeros((lax.axis_size("dp") * group_rows, 2 * columns), jnp.float32),
        tree_grads,
        tree_index * tree_len,
        0,
    )
    own_grads = lax.psum_scatter(placed, "dp", scatter_dimension=0, tiled=True)
    grad_project = jnp.concatenate([grad_query, own_grads.astype(jnp.bfloat16)], axis=1)
    grad_w_project = jnp.dot(rows_all.T, grad_project, preferred_element_type=jnp.float32)
    grad_inputs = grad_first + lax.psum_scatter(
        jnp.dot(grad_project, full_project.T, preferred_element_type=jnp.float32).astype(
            jnp.bfloat16
        ),
        "tensor",
        scatter_dimension=0,
        tiled=True,
    ).astype(jnp.float32)
    weight_grads = (
        lax.psum_scatter(grad_w_project[:, :columns], "dp", scatter_dimension=0, tiled=True),
        lax.psum_scatter(
            grad_w_project[:, columns : 2 * columns], "dp", scatter_dimension=0, tiled=True
        ),
        lax.psum_scatter(grad_w_project[:, 2 * columns :], "dp", scatter_dimension=0, tiled=True),
        lax.psum_scatter(grad_w_attn, "dp", scatter_dimension=1, tiled=True),
        lax.psum_scatter(grad_w_inner, "dp", scatter_dimension=0, tiled=True),
        lax.psum_scatter(grad_bias, "dp", scatter_dimension=0, tiled=True),
        lax.psum_scatter(grad_w_outer, "dp", scatter_dimension=0, tiled=True),
    )
    norm_grads = lax.psum(
        (grad_gain_one, grad_shift_one, grad_gain_two, grad_shift_two), ("dp", "tensor")
    )
    return (
        result.astype(jnp.bfloat16),
        logits,
        grad_inputs,
        grad_scores,
        weight_grads[0],
        weight_grads[1],
        weight_grads[2],
        weight_grads[3],
        weight_grads[4],
        weight_grads[5],
        weight_grads[6],
        norm_grads[0],
        norm_grads[1],
        norm_grads[2],
        norm_grads[3],
    )


def solution(mesh):
    placed = (
        P(("dp", "tensor"), None),
        P("dp", "tensor", None),
        P("dp", "tensor"),
        P("dp", "tensor"),
        P("dp", "tensor"),
        P("tensor", "dp"),
        P("dp", "tensor"),
        P(("tensor", "dp")),
        P(("tensor", "dp"), None),
        P(),
        P(),
        P(),
        P(),
        P(),
        P(),
        P(("dp", "tensor"), None),
        P("dp", "tensor", None),
    )
    return jax.shard_map(
        shards,
        mesh=mesh,
        in_specs=placed,
        out_specs=(
            P(("dp", "tensor"), None),
            P("dp", "tensor", None),
            P(("dp", "tensor"), None),
            P("dp", "tensor", None),
            P("dp", "tensor"),
            P("dp", "tensor"),
            P("dp", "tensor"),
            P("tensor", "dp"),
            P("dp", "tensor"),
            P(("tensor", "dp")),
            P(("tensor", "dp"), None),
            P(),
            P(),
            P(),
            P(),
        ),
        check_vma=False,
    )
```

profile of v0, /device:TPU:0, one launch (start us, length us, event | category | flops | bytes accessed | tf_op | source)
XLA Modules:
  0.0 1029.8 jit_solution(4397699468486531703)
XLA Ops:
  7.2 33.0 %all_gather.36 = bf16[768,192]{1,0:T(8,128)(2,1)S(1)} all-gather(bf16[96,192]{1,0:T(8,128)(2,1)} %param.19), channel_id=1, replica_groups=mesh['dp'=8,'tensor'=4] {'dp'}, dimensions={0}, use_global_device_ids=true | all-gather | bytes 331776 | tf_op jit(solution)/shard_map/all_gather | solution.py:130
  40.2 31.4 %all_gather.37 = bf16[768,192]{1,0:T(8,128)(2,1)S(1)} all-gather(bf16[96,192]{1,0:T(8,128)(2,1)} %param.20), channel_id=1, replica_groups=mesh['dp'=8,'tensor'=4] {'dp'}, dimensions={0}, use_global_device_ids=true | all-gather | bytes 331776 | tf_op jit(solution)/shard_map/all_gather | solution.py:131
  71.6 31.2 %all_gather.38 = bf16[768,192]{1,0:T(8,128)(2,1)S(1)} all-gather(bf16[96,192]{1,0:T(8,128)(2,1)} %param.21), channel_id=1, replica_groups=mesh['dp'=8,'tensor'=4] {'dp'}, dimensions={0}, use_global_device_ids=true | all-gather | bytes 331776 | tf_op jit(solution)/shard_map/all_gather | solution.py:132
  102.7 8.8 all_gather.39
  113.6 16.6 %copy.55 = bf16[512,3,4096]{0,2,1:T(8,128)(2,1)} copy(bf16[512,3,4096]{2,0,1:T(8,128)(2,1)} %param.18) | data formatting | bytes 25165824 | tf_op args[1]
  130.5 32.3 %all_gather.41 = bf16[192,768]{0,1:T(8,128)(2,1)S(1)} all-gather(bf16[192,96]{0,1:T(8,128)(2,1)S(1)} %copy.57), channel_id=1, replica_groups=mesh['dp'=8,'tensor'=4] {'dp'}, dimensions={1}, use_global_device_ids=true | all-gather | bytes 331776 | tf_op jit(solution)/shard_map/all_gather | solution.py:133
  166.3 14.6 %all-gather.4.cloned.1.call-done = bf16[4096,384]{0,1:T(8,128)(2,1)} async-done(((bf16[512,384]{0,1:T(8,128)(2,1)}), bf16[4096,384]{0,1:T(8,128)(2,1)}) %all-gather.4.cloned.1.call-update) | async-done | bytes 3145744 | tf_op jit(solution)/shard_map/all_gather | solution.py:145
  183.4 14.6 %select_reduce_fusion = (f32[512,3]{0,1:T(4,128)S(1)}, f32[512,3,4096]{0,2,1:T(8,128)}) fusion(pred[512,4096]{0,1:T(8,128)(4,1)S(1)} %copy-done, bf16[512,3,4096]{0,2,1:T(8,128)(2,1)} %copy.55, bf16[4096,3,64]{0,2,1:T(8,128)(2,1)S(1)} %bitcast.77, bf16[512,3,64]{0,2,1:T(8,128)(2,1)S(1)} %bitcast.85), kind=kOutput, calls=%fused_computation.13 | convolution fusion | flops 836762112 | bytes 41621504 | tf_op jit(solution)/shard_map/qhe,khe->qhk/dot_general | solution.py:30
  198.0 11.0 %fusion.5 = f32[512,3]{0,1:T(4,128)S(1)} fusion(f32[512,3,4096]{0,2,1:T(8,128)} %get-tuple-element.87, f32[512,3]{0,1:T(4,128)S(1)} %get-tuple-element.86, pred[512,4096]{0,1:T(8,128)(4,1)S(1)} %copy-done), kind=kLoop, calls=%fused_computation.12 | loop fusion | flops 18872832 | bytes 27275264 | tf_op jit(solution)/shard_map/reduce_sum | solution.py:37
  209.0 11.5 %fusion.29 = bf16[3,64,512]{2,1,0:T(8,128)(2,1)S(1)} fusion(bf16[4096,3,64]{0,2,1:T(8,128)(2,1)S(1)} %bitcast.83, f32[512,3,4096]{0,2,1:T(8,128)} %get-tuple-element.87, f32[512,3]{0,1:T(4,128)S(1)} %fusion.5, f32[512,3]{0,1:T(4,128)S(1)} %get-tuple-element.86, pred[512,4096]{0,1:T(8,128)(4,1)S(1)} %copy-done), kind=kOutput, calls=%fused_computation.63 | convolution fusion | flops 830570496 | bytes 29044736 | tf_op jit(solution)/shard_map/qhk,khe->qhe/dot_general | solution.py:41
  225.4 17.9 %all-reduce = bf16[768]{0:T(1024)(128)(2,1)S(1)} all-reduce(bf16[768]{0:T(1024)(128)(2,1)S(1)} %dynamic-update-slice), channel_id=1, replica_groups=mesh['dp'=8,'tensor'=4] {'dp'}, use_global_device_ids=true, to_apply=%add | all-reduce | flops 768 | bytes 3072
  247.1 8.4 all_gather.42
  255.5 31.8 %all-gather.6.cloned.1.call-done = bf16[768,768]{1,0:T(8,128)(2,1)} async-done(((bf16[96,768]{1,0:T(8,128)(2,1)}), bf16[768,768]{1,0:T(8,128)(2,1)}) %all-gather.6.cloned.1.call-update) | async-done | bytes 1179664 | tf_op jit(solution)/shard_map/all_gather | solution.py:134
  293.8 35.6 %all-gather.8.cloned.1.call-done = bf16[768,768]{1,0:T(8,128)(2,1)} async-done(((bf16[96,768]{1,0:T(8,128)(2,1)}), bf16[768,768]{1,0:T(8,128)(2,1)}) %all-gather.8.cloned.1.call-update) | async-done | bytes 1179664 | tf_op jit(solution)/shard_map/all_gather | solution.py:136
  332.8 22.1 %reduce-scatter.22.cloned.1.call-done = bf16[128,768]{1,0:T(8,128)(2,1)} async-done(((bf16[512,768]{1,0:T(8,128)(2,1)}), bf16[128,768]{1,0:T(8,128)(2,1)}) %reduce-scatter.22.cloned.1.call-update) | async-done | bytes 196624 | tf_op jit(solution)/shard_map/reduce_scatter | solution.py:180
  357.7 8.2 all_gather.46
  370.4 16.6 %copy.58 = bf16[512,3,4096]{0,2,1:T(8,128)(2,1)} copy(bf16[512,3,4096]{2,0,1:T(8,128)(2,1)} %param.33) | data formatting | bytes 25165824 | tf_op args[16]
  397.4 8.6 all_gather.47
  407.1 13.0 %fusion.7 = f32[3,64,4096]{2,1,0:T(8,128)} fusion(bf16[512,3,64]{0,2,1:T(8,128)(2,1)S(1)} %bitcast.89, f32[512,3,4096]{0,2,1:T(8,128)} %get-tuple-element.87, f32[512,3]{0,1:T(4,128)S(1)} %copy-done.31, pred[512,4096]{0,1:T(8,128)(4,1)S(1)} %copy-done.1), kind=kOutput, calls=%fused_computation.15 | convolution fusion | flops 824180736 | bytes 30611456 | tf_op jit(solution)/shard_map/qhk,qhe->khe/dot_general | solution.py:65
  420.1 38.9 %fusion.4 = bf16[512,3,4096]{0,2,1:T(8,128)(2,1)} fusion(bf16[512,3,4096]{0,2,1:T(8,128)(2,1)} %copy.58, f32[512,3,4096]{0,2,1:T(8,128)} %get-tuple-element.87, f32[512,3]{0,1:T(4,128)} %log_add_fusion, pred[512,4096]{0,1:T(8,128)(4,1)} %compare_or_fusion, bf16[4096,3,64]{0,2,1:T(8,128)(2,1)} %bitcast.84, bf16[512,3,64]{0,2,1:T(8,128)(2,1)} %bitcast.90), kind=kOutput, calls=%fused_computation.6 | convolution fusion | flops 1679824384 | bytes 54204416 | tf_op jit(solution)/shard_map/sub | solution.py:72
  459.0 8.7 convolution_multiply_fusion
  480.3 109.4 %reduce-scatter.26.cloned.1.call-done = f32[512,384]{0,1:T(8,128)} async-done(((f32[4096,384]{0,1:T(8,128)}), f32[512,384]{0,1:T(8,128)}) %reduce-scatter.26.cloned.1.call-update) | async-done | bytes 786448 | tf_op jit(solution)/shard_map/reduce_scatter | solution.py:229
  606.2 14.9 %select_convert_fusion = bf16[512,3,4096]{0,2,1:T(8,128)(2,1)} fusion(f32[512,3,4096]{0,2,1:T(8,128)} %get-tuple-element.87, pred[512,4096]{0,1:T(8,128)(4,1)S(1)} %copy-done.2), kind=kLoop, calls=%fused_computation.9 | loop fusion | flops 6291456 | bytes 39845888 | tf_op jit(solution)/shard_map/convert_element_type | solution.py:33
  621.1 16.9 %copy.62 = bf16[512,3,4096]{2,0,1:T(8,128)(2,1)} copy(bf16[512,3,4096]{0,2,1:T(8,128)(2,1)} %select_convert_fusion) | data formatting | bytes 25165824
  638.0 19.7 %all-reduce.1 = f32[768]{0:T(1024)S(1)} all-reduce(f32[768]{0:T(1024)S(1)} %copy-done.34), channel_id=12, replica_groups=mesh['dp'=8,'tensor'=4] {'dp'}, use_global_device_ids=true, to_apply=%region_24.25.clone | all-reduce | flops 768 | bytes 6144
  658.3 16.9 %copy.63 = bf16[512,3,4096]{2,0,1:T(8,128)(2,1)} copy(bf16[512,3,4096]{0,2,1:T(8,128)(2,1)} %fusion.4) | data formatting | bytes 25165824
  675.3 38.2 %all-reduce.2 = (f32[768]{0:T(1024)}, f32[768]{0:T(1024)}, f32[768]{0:T(1024)}, f32[768]{0:T(1024)}) all-reduce(f32[768]{0:T(1024)S(1)} %get-tuple-element.60, f32[768]{0:T(1024)S(1)} %copy-done.28, f32[768]{0:T(1024)S(1)} %get-tuple-element.62, f32[768]{0:T(1024)S(1)} %get-tuple-element.65), channel_id=1, replica_groups=mesh['dp'=8,'tensor'=4] {'dp','tensor'}, use_global_device_ids=true, to_apply=%region_27.28 | all-reduce | flops 3072 | bytes 24576 | tf_op jit(solution)/shard_map/psum | solution.py:251
  716.9 37.0 %reduce-scatter.32.cloned.1.call-done = f32[96,768]{1,0:T(8,128)} async-done(((f32[768,768]{1,0:T(8,128)}), f32[96,768]{1,0:T(8,128)}) %reduce-scatter.32.cloned.1.call-update) | async-done | bytes 294928 | tf_op jit(solution)/shard_map/reduce_scatter | solution.py:249
  754.0 72.5 %reduce-scatter.30.cloned.1.call-done = f32[96,768]{1,0:T(8,128)} async-done(((f32[768,768]{1,0:T(8,128)}), f32[96,768]{1,0:T(8,128)}) %reduce-scatter.30.cloned.1.call-update) | async-done | bytes 294928 | tf_op jit(solution)/shard_map/reduce_scatter | solution.py:247
  826.5 65.6 %reduce-scatter.38.cloned.1.call-done = f32[96,192]{1,0:T(8,128)} async-done(((f32[768,192]{1,0:T(8,128)}), f32[96,192]{1,0:T(8,128)}) %reduce-scatter.38.cloned.1.call-update) | async-done | bytes 73744
  892.0 65.3 %reduce-scatter.36.cloned.1.call-done = f32[96,192]{1,0:T(8,128)} async-done(((f32[768,192]{1,0:T(8,128)}), f32[96,192]{1,0:T(8,128)}) %reduce-scatter.36.cloned.1.call-update) | async-done | bytes 73744
  957.3 65.5 %reduce-scatter.34.cloned.1.call-done = f32[96,192]{1,0:T(8,128)} async-done(((f32[768,192]{1,0:T(8,128)}), f32[96,192]{1,0:T(8,128)}) %reduce-scatter.34.cloned.1.call-update) | async-done | bytes 73744
  (174 shorter events, 76.8 us)
Async XLA Ops:
  7.2 173.7 %all-gather.4.cloned.1.call-start = ((), (), s32[]{:S(2)}) async-start(), calls=%async_computation.11 | async-start | bytes 3538944 | tf_op jit(solution)/shard_map/all_gather | solution.py:145
  40.2 72.4 %copy-start.19 = (bf16[768,192]{1,0:T(8,128)(2,1)}, bf16[768,192]{1,0:T(8,128)(2,1)S(1)}, u32[]{:S(2)}) copy-start(bf16[768,192]{1,0:T(8,128)(2,1)S(1)} %all_gather.36) | copy-start | bytes 884740
  71.6 41.0 %copy-start.20 = (bf16[768,192]{1,0:T(8,128)(2,1)}, bf16[768,192]{1,0:T(8,128)(2,1)S(1)}, u32[]{:S(2)}) copy-start(bf16[768,192]{1,0:T(8,128)(2,1)S(1)} %all_gather.37) | copy-start | bytes 884740
  113.4 130.4 %reduce-scatter.20.cloned.1.call-start = ((), (), s32[]{:S(2)}) async-start(), calls=%async_computation.12 | async-start | bytes 983040 | tf_op jit(solution)/shard_map/reduce_scatter | solution.py:166
  113.5 69.7 %copy-start.14 = (bf16[512,192]{0,1:T(8,128)(2,1)}, bf16[512,192]{0,1:T(8,128)(2,1)S(1)}, u32[]{:S(2)}) copy-start(bf16[512,192]{0,1:T(8,128)(2,1)S(1)} %slice.33) | copy-start | bytes 589828
  162.8 57.8 %copy-start.5 = (bf16[192,768]{0,1:T(8,128)(2,1)}, bf16[192,768]{0,1:T(8,128)(2,1)S(1)}, u32[]{:S(2)}) copy-start(bf16[192,768]{0,1:T(8,128)(2,1)S(1)} %all_gather.41) | copy-start | bytes 884740
  183.2 25.8 %copy-start.13 = (bf16[4096,192]{0,1:T(8,128)(2,1)}, bf16[4096,192]{0,1:T(8,128)(2,1)S(1)}, u32[]{:S(2)}) copy-start(bf16[4096,192]{0,1:T(8,128)(2,1)S(1)} %get-tuple-element.79) | copy-start | bytes 4718596
  220.5 23.3 %copy-start.3 = (bf16[128,768]{1,0:T(8,128)(2,1)S(1)}, bf16[128,768]{1,0:T(8,128)(2,1)}, u32[]{:S(2)}) copy-start(bf16[128,768]{1,0:T(8,128)(2,1)} %param.17) | copy-start | bytes 589828
  221.2 24.8 %copy-start.23 = (f32[768]{0:T(1024)S(1)}, f32[768]{0:T(1024)}, u32[]{:S(2)}) copy-start(f32[768]{0:T(1024)} %param.26) | copy-start | bytes 9220
  221.2 24.8 %copy-start.26 = (f32[768]{0:T(1024)S(1)}, f32[768]{0:T(1024)}, u32[]{:S(2)}) copy-start(f32[768]{0:T(1024)} %param.27) | copy-start | bytes 9220
  222.5 64.8 %all-gather.6.cloned.1.call-start = ((), (), s32[]{:S(2)}) async-start(), calls=%async_computation.13 | async-start | bytes 1327104 | tf_op jit(solution)/shard_map/all_gather | solution.py:134
  223.2 106.2 %all-gather.8.cloned.1.call-start = ((), (), s32[]{:S(2)}) async-start(), calls=%async_computation.14 | async-start | bytes 1327104 | tf_op jit(solution)/shard_map/all_gather | solution.py:136
  223.8 131.1 %reduce-scatter.22.cloned.1.call-start = ((), (), s32[]{:S(2)}) async-start(), calls=%async_computation.15 | async-start | bytes 983040 | tf_op jit(solution)/shard_map/reduce_scatter | solution.py:180
  244.9 149.3 %copy-start.29 = (f32[128]{0:T(128)}, f32[128]{0:T(128)S(1)}, u32[]{:S(2)}) copy-start(f32[128]{0:T(128)S(1)} %broadcast_multiply_fusion.1) | copy-start | bytes 1540
  246.0 148.1 %copy-start.30 = (f32[128]{0:T(128)}, f32[128]{0:T(128)S(1)}, u32[]{:S(2)}) copy-start(f32[128]{0:T(128)S(1)} %fusion.39) | copy-start | bytes 1540
  329.5 25.5 %copy-start.4 = (bf16[128,768]{1,0:T(8,128)(2,1)S(1)}, bf16[128,768]{1,0:T(8,128)(2,1)}, u32[]{:S(2)}) copy-start(bf16[128,768]{1,0:T(8,128)(2,1)} %reduce-scatter.20.cloned.1.call-done) | copy-start | bytes 589828
  332.7 23.7 %copy-start.15 = (bf16[128,768]{1,0:T(8,128)(2,1)S(1)}, bf16[128,768]{1,0:T(8,128)(2,1)}, u32[]{:S(2)}) copy-start(bf16[128,768]{1,0:T(8,128)(2,1)} %param.32) | copy-start | bytes 589828
  332.7 23.7 %copy-start.27 = (f32[768]{0:T(1024)S(1)}, f32[768]{0:T(1024)}, u32[]{:S(2)}) copy-start(f32[768]{0:T(1024)} %param.28) | copy-start | bytes 9220
  332.7 24.0 %copy-start.33 = (f32[768]{0:T(1024)S(1)}, f32[768]{0:T(1024)}, u32[]{:S(2)}) copy-start(f32[768]{0:T(1024)} %param.29) | copy-start | bytes 9220
  332.7 61.4 %reduce-scatter.24.cloned.1.call-start = ((), (), s32[]{:S(2)}) async-start(), calls=%async_computation.16 | async-start | bytes 983040 | tf_op jit(solution)/shard_map/reduce_scatter | solution.py:197
  357.6 36.5 %copy-start.32 = (f32[128]{0:T(128)}, f32[128]{0:T(128)S(1)}, u32[]{:S(2)}) copy-start(f32[128]{0:T(128)S(1)} %negate_multiply_fusion.2) | copy-start | bytes 1540
  370.3 219.4 %reduce-scatter.26.cloned.1.call-start = ((), (), s32[]{:S(2)}) async-start(), calls=%async_computation.17 | async-start | bytes 7077888 | tf_op jit(solution)/shard_map/reduce_scatter | solution.py:229
  397.3 22.8 %copy-start.35 = (f32[128]{0:T(128)}, f32[128]{0:T(128)S(1)}, u32[]{:S(2)}) copy-start(f32[128]{0:T(128)S(1)} %negate_multiply_fusion.1) | copy-start | bytes 1540
  470.8 242.7 %reduce-scatter.40.cloned.1.call-start = ((), (), s32[]{:S(2)}) async-start(), calls=%async_computation.24 | async-start | bytes 884736
  473.1 242.0 %reduce-scatter.28.cloned.1.call-start = ((), (), s32[]{:S(2)}) async-start(), calls=%async_computation.18 | async-start | bytes 983040 | tf_op jit(solution)/shard_map/reduce_scatter | solution.py:232
  594.2 159.8 %reduce-scatter.32.cloned.1.call-start = ((), (), s32[]{:S(2)}) async-start(), calls=%async_computation.20 | async-start | bytes 2654208 | tf_op jit(solution)/shard_map/reduce_scatter | solution.py:249
  596.5 230.0 %reduce-scatter.30.cloned.1.call-start = ((), (), s32[]{:S(2)}) async-start(), calls=%async_computation.19 | async-start | bytes 2654208 | tf_op jit(solution)/shard_map/reduce_scatter | solution.py:247
  599.9 292.2 %reduce-scatter.38.cloned.1.call-start = ((), (), s32[]{:S(2)}) async-start(), calls=%async_computation.23 | async-start | bytes 884736
  602.9 354.4 %reduce-scatter.36.cloned.1.call-start = ((), (), s32[]{:S(2)}) async-start(), calls=%async_computation.22 | async-start | bytes 884736
  604.2 418.7 %reduce-scatter.34.cloned.1.call-start = ((), (), s32[]{:S(2)}) async-start(), calls=%async_computation.21 | async-start | bytes 884736
  658.3 16.9 %copy-start.28 = (f32[768]{0:T(1024)S(1)}, f32[768]{0:T(1024)}, u32[]{:S(2)}) copy-start(f32[768]{0:T(1024)} %get-tuple-element.64) | copy-start | bytes 9220
  658.3 56.8 %copy-start.36 = (f32[128]{0:T(128)S(1)}, f32[128]{0:T(128)}, u32[]{:S(2)}) copy-start(f32[128]{0:T(128)} %copy-done.35) | copy-start | bytes 1540
  (26 other events, 158.8 us)
Sparse Core Ops, SparseCore 0:
  113.5 67.3 all-gather.3
  222.6 21.1 reduce-scatter.19
  246.2 41.0 all-gather.5
  289.6 39.8 all-gather.7
  332.9 21.9 reduce-scatter.21
  370.4 23.6 reduce-scatter.23
  470.9 118.7 reduce-scatter.25
  593.3 61.6 reduce-scatter.39
  657.5 22.2 reduce-scatter.27
  684.1 69.7 reduce-scatter.31
  758.4 68.0 reduce-scatter.29
  830.6 61.4 reduce-scatter.37
  895.9 61.3 reduce-scatter.35
  961.4 61.3 reduce-scatter.33
where the time goes:
time: 1040 us; the launch traced here: 1030 us
  waiting for transfers between devices  528 us (51%)
  blocking collectives  238 us (23%)
  matrix products  120 us (12%)
  local copies, waits for them, and re-layouts  81.7 us (8%)
  other arithmetic  45.5 us (4%)
  between operations  16.3 us (2%)
    unnamed x18, waiting for transfers between devices  198 us
    reduce_scatter x1, waiting for transfers between devices, shards(): own_grads = lax.psum_scatter(placed, 'dp', scatter_dimension=0, tiled=True)  109 us
    unnamed x101, local copies, waits for them, and re-layouts  78.4 us
    reduce_scatter x1, waiting for transfers between devices, shards(): lax.psum_scatter(grad_w_inner, 'dp', scatter_dimension=0, tiled=True)  72.5 us
    sub x1, matrix products, run(): grad_weight - jnp.sum(attention_weight * grad_weight, axis=-1, keepdims=T...  38.9 us
    psum x1, blocking collectives, shards(): lax.psum((grad_gain_one, grad_shift_one, grad_gain_two, grad_shift_two),...  38.2 us
    unnamed x2, blocking collectives  37.6 us
    reduce_scatter x1, waiting for transfers between devices, shards(): lax.psum_scatter(grad_w_outer, 'dp', scatter_dimension=0, tiled=True)  37 us
  transfers between devices with their start and end apart: 14, of which 12 were waited for; matrix products, arithmetic and copies ran while one was open for 12% of the time, Pallas kernels for 0%

commit v1 on v0

v1 whole, which is shorter than its diff:
```python
import functools

import jax
import jax.numpy as jnp
from jax import lax
from jax.experimental import pallas as pl
from jax.experimental.pallas import tpu as pltpu
from jax.sharding import PartitionSpec as P

E = 64
TRUNK = 2048
BLOCK = 128
EPSILON = 1e-12
LOW = -1e30

BF = jnp.bfloat16
F32 = jnp.float32


def layer_norm(values, norm_gain, norm_shift):
    center = values - jnp.mean(values, axis=-1, keepdims=True)
    spread = jnp.mean(center * center, axis=-1, keepdims=True)
    return center * lax.rsqrt(spread + EPSILON) * norm_gain + norm_shift


def contract(a, b, da, db):
    return lax.dot_general(a, b, (((da,), (db,)), ((), ())), preferred_element_type=F32)


def forward_kernel(sid_ref, rid_ref, act_ref, q_ref, kv_ref, prev_ref, logit_ref, mix_ref, aux_ref, m_s, l_s, acc_s, q_s):
    j = pl.program_id(1)
    rows = prev_ref.shape[1]
    nb = rows // BLOCK
    chunk = min(256, rows)
    total_blocks = act_ref.shape[0] // nb
    shard = sid_ref[j]

    @pl.when(j == 0)
    def _():
        m_s[...] = jnp.full(m_s.shape, LOW, F32)
        l_s[...] = jnp.zeros(l_s.shape, F32)
        acc_s[...] = jnp.zeros(acc_s.shape, F32)
        q_s[...] = q_ref[...].astype(F32).T.astype(BF)

    def update(r0, count, s, vt):
        rs = pl.ds(r0, count)
        m_old = m_s[rs, :]
        m_new = jnp.maximum(m_old, jnp.max(s, axis=1, keepdims=True))
        p = jnp.exp(s - m_new)
        fix = jnp.exp(m_old - m_new)
        m_s[rs, :] = m_new
        l_s[rs, :] = l_s[rs, :] * fix + jnp.sum(p, axis=1, keepdims=True)
        acc_s[rs, :] = acc_s[rs, :] * fix + contract(p.astype(BF), vt, 1, 1)

    dense = (shard + 1) * rows <= TRUNK

    @pl.when(dense)
    def _():
        for r0 in range(0, rows, chunk):
            s = contract(q_s[r0 : r0 + chunk, :], kv_ref[0, 0], 1, 0)
            s = s + prev_ref[0, r0 : r0 + chunk, :].astype(F32)
            logit_ref[0, r0 : r0 + chunk, :] = s.astype(BF)
            update(r0, chunk, s, kv_ref[0, 1])

    @pl.when(jnp.logical_not(dense))
    def _():
        logit_ref[...] = jnp.zeros(logit_ref.shape, BF)
        for qi in range(nb):
            for ki in range(nb):

                @pl.when(act_ref[qi * total_blocks + shard * nb + ki] == 1)
                def _(qi=qi, ki=ki):
                    r0, c0 = qi * BLOCK, ki * BLOCK
                    s = contract(q_s[r0 : r0 + BLOCK, :], kv_ref[0, 0, :, c0 : c0 + BLOCK], 1, 0)
                    s = s + prev_ref[0, r0 : r0 + BLOCK, c0 : c0 + BLOCK].astype(F32)
                    logit_ref[0, r0 : r0 + BLOCK, c0 : c0 + BLOCK] = s.astype(BF)
                    update(r0, BLOCK, s, kv_ref[0, 1, :, c0 : c0 + BLOCK])

    @pl.when(j == pl.num_programs(1) - 1)
    def _():
        out = acc_s[...] / l_s[...]
        mix_ref[...] = out.T.astype(BF)
        aux_ref[0, :, :E] = out
        aux_ref[0, :, E:] = jnp.broadcast_to(m_s[...] + jnp.log(l_s[...]), (rows, 128 - E))


def attend_forward(sid, rid, act, q_t, kv, prev):
    heads, rows, length = prev.shape
    pieces = kv.shape[0]
    return pl.pallas_call(
        forward_kernel,
        out_shape=(
            jax.ShapeDtypeStruct((heads, rows, length), BF),
            jax.ShapeDtypeStruct((heads * E, rows), BF),
            jax.ShapeDtypeStruct((heads, rows, 128), F32),
        ),
        grid_spec=pltpu.PrefetchScalarGridSpec(
            num_scalar_prefetch=3,
            grid=(heads, pieces),
            in_specs=[
                pl.BlockSpec((E, rows), lambda h, j, s, r, a: (h, 0)),
                pl.BlockSpec((1, 2, E, rows), lambda h, j, s, r, a: (j, 0, h, 0)),
                pl.BlockSpec((1, rows, rows), lambda h, j, s, r, a: (h, 0, r[j])),
            ],
            out_specs=[
                pl.BlockSpec((1, rows, rows), lambda h, j, s, r, a: (h, 0, s[j])),
                pl.BlockSpec((E, rows), lambda h, j, s, r, a: (h, 0)),
                pl.BlockSpec((1, rows, 128), lambda h, j, s, r, a: (h, 0, 0)),
            ],
            scratch_shapes=[
                pltpu.VMEM((rows, 1), F32),
                pltpu.VMEM((rows, 1), F32),
                pltpu.VMEM((rows, E), F32),
                pltpu.VMEM((rows, E), BF),
            ],
        ),
        compiler_params=pltpu.CompilerParams(dimension_semantics=("arbitrary", "arbitrary")),
    )(sid, rid, act, q_t, kv, prev)


def backward_kernel(sid_ref, rid_ref, act_ref, q_ref, kv_ref, prev_ref, up_ref, aux_ref, do_ref, pg_ref, gkv_ref, gq_ref, q_s, do_s, d_s, lse_s, gq_s, p_s):
    j = pl.program_id(1)
    rows = prev_ref.shape[1]
    nb = rows // BLOCK
    chunk = min(256, rows)
    total_blocks = act_ref.shape[0] // nb
    shard = sid_ref[j]

    @pl.when(j == 0)
    def _():
        q_s[...] = q_ref[...].astype(F32).T.astype(BF)
        do = do_ref[...].astype(F32).T
        do_s[...] = do.astype(BF)
        d_s[...] = jnp.sum(do * aux_ref[0, :, :E], axis=1, keepdims=True)
        lse_s[...] = aux_ref[0, :, E : E + 1]
        gq_s[...] = jnp.zeros(gq_s.shape, F32)

    def fill(r0, count, c0, width):
        rs, cs = slice(r0, r0 + count), slice(c0, c0 + width)
        s = contract(q_s[rs, :], kv_ref[0, 0, :, cs], 1, 0) + prev_ref[0, rs, cs].astype(F32)
        p = jnp.exp(s - lse_s[rs, :])
        dp = contract(do_s[rs, :], kv_ref[0, 1, :, cs], 1, 0)
        ds = p * (dp - d_s[rs, :]) + up_ref[0, rs, cs].astype(F32)
        pg_ref[0, rs, cs] = ds.astype(BF)
        p_s[rs, cs] = p.astype(BF)

    def finish():
        gkv_ref[0, 0] = contract(q_ref[...], pg_ref[0], 1, 0).astype(BF)
        gkv_ref[0, 1] = contract(do_ref[...], p_s[...], 1, 0).astype(BF)
        gq_s[...] += contract(pg_ref[0], kv_ref[0, 0], 1, 1)

    dense = (shard + 1) * rows <= TRUNK

    @pl.when(dense)
    def _():
        for r0 in range(0, rows, chunk):
            fill(r0, chunk, 0, rows)
        finish()

    @pl.when(jnp.logical_not(dense))
    def _():
        pg_ref[...] = jnp.zeros(pg_ref.shape, BF)
        some = act_ref[shard * nb]
        for qi in range(nb):
            for ki in range(nb):
                some = jnp.maximum(some, act_ref[qi * total_blocks + shard * nb + ki])

        @pl.when(some == 0)
        def _():
            gkv_ref[...] = jnp.zeros(gkv_ref.shape, BF)

        @pl.when(some == 1)
        def _():
            p_s[...] = jnp.zeros(p_s.shape, BF)
            for qi in range(nb):
                for ki in range(nb):

                    @pl.when(act_ref[qi * total_blocks + shard * nb + ki] == 1)
                    def _(qi=qi, ki=ki):
                        fill(qi * BLOCK, BLOCK, ki * BLOCK, BLOCK)

            finish()

    @pl.when(j == pl.num_programs(1) - 1)
    def _():
        gq_ref[...] = (gq_s[...] * (E ** (-0.5))).T.astype(BF)


def attend_backward(sid, rid, act, q_t, kv, prev, up, aux, do_t):
    heads, rows, length = prev.shape
    pieces = kv.shape[0]
    return pl.pallas_call(
        backward_kernel,
        out_shape=(
            jax.ShapeDtypeStruct((heads, rows, length), BF),
            jax.ShapeDtypeStruct((pieces, 2, heads * E, rows), BF),
            jax.ShapeDtypeStruct((heads * E, rows), BF),
        ),
        grid_spec=pltpu.PrefetchScalarGridSpec(
            num_scalar_prefetch=3,
            grid=(heads, pieces),
            in_specs=[
                pl.BlockSpec((E, rows), lambda h, j, s, r, a: (h, 0)),
                pl.BlockSpec((1, 2, E, rows), lambda h, j, s, r, a: (j, 0, h, 0)),
                pl.BlockSpec((1, rows, rows), lambda h, j, s, r, a: (h, 0, r[j])),
                pl.BlockSpec((1, rows, rows), lambda h, j, s, r, a: (h, 0, r[j])),
                pl.BlockSpec((1, rows, 128), lambda h, j, s, r, a: (h, 0, 0)),
                pl.BlockSpec((E, rows), lambda h, j, s, r, a: (h, 0)),
            ],
            out_specs=[
                pl.BlockSpec((1, rows, rows), lambda h, j, s, r, a: (h, 0, s[j])),
                pl.BlockSpec((1, 2, E, rows), lambda h, j, s, r, a: (j, 0, h, 0)),
                pl.BlockSpec((E, rows), lambda h, j, s, r, a: (h, 0)),
            ],
            scratch_shapes=[
                pltpu.VMEM((rows, E), BF),
                pltpu.VMEM((rows, E), BF),
                pltpu.VMEM((rows, 1), F32),
                pltpu.VMEM((rows, 1), F32),
                pltpu.VMEM((rows, E), F32),
                pltpu.VMEM((rows, rows), BF),
            ],
        ),
        compiler_params=pltpu.CompilerParams(dimension_semantics=("arbitrary", "arbitrary")),
    )(sid, rid, act, q_t, kv, prev, up, aux, do_t)


class Ring:
    def __init__(self, axis, total, size):
        self.axis, self.size = axis, size
        local = list(range(0, size, 2)) + list(range(size - 1 - size % 2, 0, -2))
        self.local = local
        self.up, self.down = [], []
        for base in range(0, total, size):
            for i in range(size):
                a, b = base + local[i], base + local[(i + 1) % size]
                self.up.append((a, b))
                self.down.append((b, a))

    def position(self, index):
        place = [0] * self.size
        for i, v in enumerate(self.local):
            place[v] = i
        return jnp.array(place, jnp.int32)[index % self.size]

    def offsets(self):
        out = [0]
        for k in range(1, self.size // 2):
            out += [-k, k]
        if self.size > 1:
            out.append(-(self.size // 2))
        return out

    def gather(self, x, split):
        pieces = [x]
        up = down = x
        for _ in range(1, self.size // 2):
            up = lax.ppermute(up, self.axis, self.up)
            down = lax.ppermute(down, self.axis, self.down)
            pieces += [up, down]
        if self.size > 1:
            half = x.shape[split] // 2
            a = lax.slice_in_dim(up, 0, half, axis=split)
            b = lax.slice_in_dim(down, half, x.shape[split], axis=split)
            a = lax.ppermute(a, self.axis, self.up)
            b = lax.ppermute(b, self.axis, self.down)
            pieces.append(jnp.concatenate([a, b], axis=split))
        return pieces

    def scatter(self, get):
        n = self.size
        up, down = get(-1 % n, 0), get(1 % n, 1)
        if n == 1:
            return up, down
        for k in range(1, n):
            up = lax.ppermute(up, self.axis, self.up_from())
            down = lax.ppermute(down, self.axis, self.down_from())
            up = (up.astype(F32) + get((-1 - k) % n, 0).astype(F32)).astype(BF)
            down = (down.astype(F32) + get((1 + k) % n, 1).astype(F32)).astype(BF)
        return up, down

    def up_from(self):
        return self.up

    def down_from(self):
        return self.down


def spread_gather(x, axis, n):
    return lax.all_to_all(jnp.broadcast_to(x[None], (n,) + x.shape), axis, 0, 0, tiled=True)


def group_sum(x, axis, n):
    parts = lax.all_to_all(x.reshape(n, x.shape[0] // n, x.shape[1]), axis, 0, 0, tiled=True)
    return jnp.sum(parts.astype(F32), axis=0)


def high_low(x):
    high = x.astype(BF)
    return high, (x - high.astype(F32)).astype(BF)


def shards(
    inputs,
    prev_logits,
    w_query,
    w_key,
    w_value,
    w_attn_out,
    w_ffn_in,
    ffn_bias,
    w_ffn_out,
    norm1_gain,
    norm1_shift,
    norm2_gain,
    norm2_shift,
    token_segment,
    segment_parent,
    out_grad,
    logit_grad,
):
    rows, heads, length = prev_logits.shape
    width = heads * E
    model = inputs.shape[1]
    own = inputs.shape[0]
    spread = length // rows
    nd, nt = lax.axis_size("dp"), lax.axis_size("tensor")
    data_index, tensor_index = lax.axis_index("dp"), lax.axis_index("tensor")
    tree_index, local_index = data_index // spread, data_index % spread
    nb = rows // BLOCK

    pack = jnp.concatenate([w_query, w_key, w_value, w_attn_out.T], axis=1)
    pack = spread_gather(pack, "dp", nd).reshape(model, 4 * width)
    project = pack[:, : 3 * width]
    out_own = pack[:, 3 * width :].T
    out_full = lax.all_gather(out_own, "tensor", axis=0, tiled=True)
    rows_all = lax.all_gather(inputs, "tensor", axis=0, tiled=True)
    w_in = lax.all_gather(w_ffn_in, "dp", axis=0, tiled=True)
    w_out = lax.all_gather(w_ffn_out, "dp", axis=0, tiled=True)
    bias = spread_gather(ffn_bias.reshape(1, -1), "dp", nd).reshape(1, -1).astype(F32)

    seg = lax.dynamic_slice_in_dim(token_segment, tree_index * length, length, 0)[::BLOCK]
    parents = lax.dynamic_slice_in_dim(segment_parent, tree_index, 1, 0)[0]
    seg_rows = lax.dynamic_slice_in_dim(seg, local_index * nb, nb, 0)
    labels = jnp.arange(parents.shape[0], dtype=jnp.int32)
    one = jnp.sum(jnp.where(seg_rows[:, None] == labels[None, :], parents[None, :], 0), axis=1)
    two = jnp.sum(jnp.where(one[:, None] == labels[None, :], parents[None, :], 0), axis=1)
    act = (
        (seg[None, :] == seg_rows[:, None])
        | (seg[None, :] == one[:, None])
        | (seg[None, :] == two[:, None])
    )
    act = act.astype(jnp.int32).reshape(-1)

    projected = contract(project, rows_all, 0, 1)
    q_t = (projected[:width] * (E ** (-0.5))).astype(BF)
    kv_own = projected[width:].astype(BF).reshape(2, width, rows)
    ring = Ring("dp", nd, spread)
    kv = jnp.stack(ring.gather(kv_own, 1), axis=0)
    place = ring.position(local_index)
    offsets = jnp.array(ring.offsets(), jnp.int32)
    local_of = jnp.array(ring.local, jnp.int32)
    sid = local_of[(place + offsets) % spread]

    prev = jnp.transpose(prev_logits, (1, 0, 2))
    up = jnp.transpose(logit_grad, (1, 0, 2))
    logits, mixed, aux = attend_forward(sid, sid, act, q_t, kv, prev)

    mixed_all = lax.all_gather(mixed, "tensor", axis=0, tiled=True)
    attended = contract(mixed_all, out_full, 0, 0)
    first_all = rows_all.astype(F32) + attended
    hidden_all = layer_norm(first_all, norm1_gain, norm1_shift).astype(BF)
    first_sum = lax.dynamic_slice_in_dim(first_all, tensor_index * own, own, 0)
    hidden, norm_one_back = jax.vjp(layer_norm, first_sum, norm1_gain, norm1_shift)

    inner = contract(hidden_all, w_in, 1, 0) + bias
    active, gelu_back = jax.vjp(lambda v: jax.nn.gelu(v, approximate=False), inner)
    active = active.astype(BF)
    ffn_out = group_sum(contract(active, w_out, 1, 0).astype(BF), "tensor", nt)
    result, norm_two_back = jax.vjp(layer_norm, hidden + ffn_out, norm2_gain, norm2_shift)
    grad_second, gain_two, shift_two = norm_two_back(out_grad.astype(F32))
    second_all = lax.all_gather(grad_second.astype(BF), "tensor", axis=0, tiled=True)
    grad_active = contract(second_all, w_out, 1, 1).astype(BF)
    grad_w_out = contract(active, second_all, 0, 0).astype(BF)
    (grad_inner,) = gelu_back(grad_active.astype(F32))
    grad_inner = grad_inner.astype(BF)
    grad_w_in = contract(hidden_all, grad_inner, 0, 0).astype(BF)
    grad_bias = jnp.sum(grad_inner.astype(F32), axis=0)
    grad_hidden = grad_second + group_sum(contract(grad_inner, w_in, 1, 1).astype(BF), "tensor", nt)
    grad_first, gain_one, shift_one = norm_one_back(grad_hidden)
    norms = jnp.stack([gain_one, shift_one, gain_two, shift_two])
    norm_high, norm_low = high_low(norms)
    gathered = lax.all_gather(
        jnp.concatenate([grad_first.astype(BF), norm_high, norm_low], axis=0), "tensor", axis=0
    )
    first_back = gathered[:, :own].reshape(nt * own, model)
    norms = jnp.sum(gathered[:, own:].astype(F32), axis=0)
    norms = norms[:4] + norms[4:]
    grad_mixed = contract(out_own, first_back, 1, 1).astype(BF)
    grad_w_attn = contract(first_back, mixed, 0, 1).astype(BF)
    rest = jnp.concatenate([grad_w_in, grad_w_attn], axis=1)
    rest = lax.psum_scatter(rest, "dp", scatter_dimension=0, tiled=True).astype(F32)
    grad_w_out = lax.psum_scatter(grad_w_out, "dp", scatter_dimension=0, tiled=True).astype(F32)

    prev_grad, grad_kv, grad_query = attend_backward(sid, sid, act, q_t, kv, prev, up, aux, grad_mixed)

    order = {o % spread: i for i, o in enumerate(ring.offsets())}
    half = width // 2

    def part(d, which):
        return grad_kv[order[d], :, which * half : (which + 1) * half]

    top, bottom = ring.scatter(part)
    own_kv = jnp.concatenate([top, bottom], axis=1).reshape(2 * width, rows)
    grad_project = jnp.concatenate([grad_query, own_kv], axis=0)

    input_part = contract(grad_project, project, 0, 1).astype(BF)
    grad_inputs = grad_first + group_sum(input_part, "tensor", nt)
    grad_w_project = contract(rows_all, grad_project, 0, 1).astype(BF)

    share = model // nd
    cols = 3 * width
    norm_high, norm_low = high_low(norms)
    bias_high, bias_low = high_low(grad_bias.reshape(nd, 1, -1))
    extra = -(-model // cols)
    small = jnp.concatenate([norm_high, norm_low], axis=0)
    small = jnp.pad(small, ((0, 0), (0, extra * cols - model))).reshape(8 * extra, cols)
    small = jnp.broadcast_to(small[None], (nd, 8 * extra, cols))
    biases = jnp.concatenate([bias_high, bias_low], axis=2)
    biases = jnp.pad(biases, ((0, 0), (0, 15), (0, cols - biases.shape[2])))
    packed = jnp.concatenate([grad_w_project.reshape(nd, share, cols), small, biases], axis=1)
    packed = lax.all_to_all(packed, "dp", 0, 0, tiled=True)
    packed = jnp.sum(packed.astype(F32), axis=0)
    w_grads = packed[:share]
    norms = packed[share : share + 8 * extra].reshape(8, extra * cols)[:, :model]
    norms = norms[:4] + norms[4:]
    nbias = grad_bias.shape[0] // nd
    biases = packed[share + 8 * extra, : 2 * nbias]
    grad_bias = biases[:nbias] + biases[nbias:]
    return (
        result.astype(BF),
        jnp.transpose(logits, (1, 0, 2)),
        grad_inputs,
        jnp.transpose(prev_grad, (1, 0, 2)),
        w_grads[:, :width],
        w_grads[:, width : 2 * width],
        w_grads[:, 2 * width :],
        rest[:, grad_w_in.shape[1] :].T,
        rest[:, : grad_w_in.shape[1]],
        grad_bias,
        grad_w_out,
        norms[0],
        norms[1],
        norms[2],
        norms[3],
    )


def solution(mesh):
    placed = (
        P(("dp", "tensor"), None),
        P("dp", "tensor", None),
        P("dp", "tensor"),
        P("dp", "tensor"),
        P("dp", "tensor"),
        P("tensor", "dp"),
        P("dp", "tensor"),
        P(("tensor", "dp")),
        P(("tensor", "dp"), None),
        P(),
        P(),
        P(),
        P(),
        P(),
        P(),
        P(("dp", "tensor"), None),
        P("dp", "tensor", None),
    )
    return jax.shard_map(
        shards,
        mesh=mesh,
        in_specs=placed,
        out_specs=(
            P(("dp", "tensor"), None),
            P("dp", "tensor", None),
            P(("dp", "tensor"), None),
            P("dp", "tensor", None),
            P("dp", "tensor"),
            P("dp", "tensor"),
            P("dp", "tensor"),
            P("tensor", "dp"),
            P("dp", "tensor"),
            P(("tensor", "dp")),
            P(("tensor", "dp"), None),
            P(),
            P(),
            P(),
            P(),
        ),
        check_vma=False,
    )
```

time: 1040 us -> 446 us (0.43)
  waiting for transfers between devices: 528 us -> 175 us
  blocking collectives: 238 us -> 72.7 us
  matrix products: 120 us -> 25.8 us
  Pallas kernels: 0 us -> 56.5 us
  local copies, waits for them, and re-layouts: 81.7 us -> 27.3 us
  starting transfers between devices: 0.83 us -> 49.7 us
  other arithmetic: 45.5 us -> 21.2 us
    reduce_scatter x7 -> x1, waiting for transfers between devices: 248 us -> 0.01 us  [shards(): lax.psum_scatter(grad_w_out, 'dp', scatter_dimension=0, tiled=True)]
    unnamed x18 -> x6, waiting for transfers between devices: 198 us -> 61.1 us
    all_gather x7 -> x3, blocking collectives: 153 us -> 25.4 us  [the longest x1 9.01 us: shards(): mixed_all = lax.all_gather(mixed, 'tensor', axis=0, tiled=True)]
    ppermute x0 -> x22, waiting for transfers between devices: none -> 82.6 us  [the longest x3 32.5 us: gather(): down = lax.ppermute(down, self.axis, self.down)]
    all_gather x3, waiting for transfers between devices: 82 us -> 0.03 us  [the longest x1 0.02 us: shards(): w_in = lax.all_gather(w_ffn_in, 'dp', axis=0, tiled=True)]
    unnamed x101 -> x86, local copies, waits for them, and re-layouts: 78.4 us -> 15 us
    pallas_call x0 -> x2, Pallas kernels: none -> 56.5 us  [the longest x1 29.4 us: attend_backward(): pl.pallas_call(backward_kernel, out_shape=(jax.ShapeDtypeStruct((heads, r...]
    dot_general x16 -> x12, matrix products: 78.9 us -> 25.8 us  [contract(): lax.dot_general(a, b, (((da,), (db,)), ((), ())), preferred_element_type=...]
  transfers between devices with their start and end apart: 14 -> 32, of which waited for: 12 -> 23; matrix products, arithmetic and copies ran while one was open for 12% -> 11% of each run, Pallas kernels for 0% -> 6%
where the time goes in v1:
time: 446 us; the launch traced here: 443 us
  waiting for transfers between devices  175 us (39%)
  blocking collectives  72.7 us (16%)
  Pallas kernels  56.5 us (13%)
  starting transfers between devices  49.7 us (11%)
  local copies, waits for them, and re-layouts  27.3 us (6%)
  matrix products  25.8 us (6%)
  other arithmetic  21.2 us (5%)
  between operations  14.6 us (3%)
    unnamed x6, waiting for transfers between devices  61.1 us
    all_to_all x1, blocking collectives, spread_gather(): lax.all_to_all(jnp.broadcast_to(x[None], (n,) + x.shape), axis, 0, 0, til...  36 us
    ppermute x3, waiting for transfers between devices, gather(): down = lax.ppermute(down, self.axis, self.down)  32.5 us
    all_to_all x3, waiting for transfers between devices, group_sum(): lax.all_to_all(x.reshape(n, x.shape[0] // n, x.shape[1]), axis, 0, 0, til...  31 us
    pallas_call x1, Pallas kernels, attend_backward(): pl.pallas_call(backward_kernel, out_shape=(jax.ShapeDtypeStruct((heads, r...  29.4 us
    pallas_call x1, Pallas kernels, attend_forward(): pl.pallas_call(forward_kernel, out_shape=(jax.ShapeDtypeStruct((heads, ro...  27.1 us
    dot_general x12, matrix products, contract(): lax.dot_general(a, b, (((da,), (db,)), ((), ())), preferred_element_type=...  25.8 us
    ppermute x7, waiting for transfers between devices, scatter(): up = lax.ppermute(up, self.axis, self.up_from())  23.5 us
  transfers between devices with their start and end apart: 32, of which 23 were waited for; matrix products, arithmetic and copies ran while one was open for 11% of the time, Pallas kernels for 6%

profile of v1, /device:TPU:0, one launch (start us, length us, event | category | flops | bytes accessed | tf_op | source)
XLA Modules:
  0.0 442.7 jit_solution(9975789252187076131)
XLA Ops:
  11.1 36.0 %all_to_all.30 = bf16[8,96,768]{2,1,0:T(8,128)(2,1)S(1)} all-to-all(bf16[8,96,768]{2,1,0:T(8,128)(2,1)S(1)} %broadcast_in_dim.40), channel_id=1, replica_groups=mesh['dp'=8,'tensor'=4] {'dp'}, dimensions={0} | all-to-all | bytes 2359296 | tf_op jit(solution)/shard_map/all_to_all | solution.py:290
  49.6 3.3 all-to-all-start.1
  56.9 11.2 %all_gather.24 = bf16[512,768]{1,0:T(8,128)(2,1)S(1)} all-gather(bf16[128,768]{1,0:T(8,128)(2,1)S(1)} %copy-done.14), channel_id=1, replica_groups=mesh['dp'=8,'tensor'=4] {'tensor'}, dimensions={0}, use_global_device_ids=true | all-gather | bytes 983040 | tf_op jit(solution)/shard_map/all_gather | solution.py:337
  75.6 8.7 %collective-permute-done.1 = bf16[2,192,512]{2,1,0:T(8,128)(2,1)} collective-permute-done((bf16[2,192,512]{2,1,0:T(8,128)(2,1)S(1)}, bf16[2,192,512]{2,1,0:T(8,128)(2,1)}, u32[]{:S(2)}, u32[]{:S(2)}) %collective-permute-start.1) | collective-permute-done | bytes 393248 | tf_op jit(solution)/shard_map/ppermute | solution.py:259
  89.7 7.2 %collective-permute-done.3 = bf16[2,192,512]{2,1,0:T(8,128)(2,1)S(1)} collective-permute-done((bf16[2,192,512]{2,1,0:T(8,128)(2,1)}, bf16[2,192,512]{2,1,0:T(8,128)(2,1)S(1)}, u32[]{:S(2)}, u32[]{:S(2)}) %collective-permute-start.3) | collective-permute-done | bytes 393248 | tf_op jit(solution)/shard_map/ppermute | solution.py:259
  99.0 16.6 %collective-permute-done.5 = bf16[2,192,512]{2,1,0:T(8,128)(2,1)S(1)} collective-permute-done((bf16[2,192,512]{2,1,0:T(8,128)(2,1)S(1)}, bf16[2,192,512]{2,1,0:T(8,128)(2,1)S(1)}, u32[]{:S(2)}, u32[]{:S(2)}) %collective-permute-start.5) | collective-permute-done | bytes 393248 | tf_op jit(solution)/shard_map/ppermute | solution.py:259
  117.8 3.9 collective-permute-done.7
  123.7 27.1 %shard_map.307 = (bf16[3,512,4096]{2,1,0:T(8,128)(2,1)}, bf16[192,512]{1,0:T(8,128)(2,1)}, f32[3,512,128]{2,1,0:T(8,128)}) custom-call(s32[8]{0:T(128)} %gather_fusion, s32[8]{0:T(128)} %gather_fusion, s32[128]{0:T(128)} %reshape.258.act_ref, bf16[192,512]{1,0:T(8,128)(2,1)} %fusion.21.q_ref, bf16[8,2,192,512]{3,2,1,0:T(8,128)(2,1)} %copy-done.1, ...), custom_call_target="tpu_custom_call" | custom-call | tf_op jit(solution)/shard_map/pallas_call | solution.py:90
  150.8 9.0 %all_gather.25 = bf16[768,512]{1,0:T(8,128)(2,1)S(1)} all-gather(bf16[192,512]{1,0:T(8,128)(2,1)} %get-tuple-element.21), channel_id=1, replica_groups=mesh['dp'=8,'tensor'=4] {'tensor'}, dimensions={0}, use_global_device_ids=true | all-gather | bytes 983040 | tf_op jit(solution)/shard_map/all_gather | solution.py:369
  162.9 6.6 %multiply_convert_fusion = (bf16[512,768]{1,0:T(8,128)(2,1)S(1)}, f32[512,768]{1,0:T(8,128)}, f32[512,768]{1,0:T(8,128)}) fusion(f32[768]{0:T(1024)S(1)} %copy-done.19, bf16[768,768]{1,0:T(8,128)(2,1)} %all-gather.7.cloned.1.call-done, f32[512,768]{1,0:T(8,128)S(1)} %get-tuple-element.174, f32[768]{0:T(1024)S(1)} %copy-done.18, f32[768]{0:T(1024)S(1)} %copy-done.15, ...), kind=kOutput, calls=%fused_computation.17 | convolution fusion | flops 631898112 | bytes 6697984 | tf_op jit(solution)/shard_map/dot_general | solution.py:27
  169.6 3.2 convolution_convert_fusion.5
  172.8 3.7 all-to-all-start.2
  176.8 11.1 %all-to-all-done.2 = bf16[4,128,768]{2,1,0:T(8,128)(2,1)S(1)} async-done(((bf16[4,128,768]{2,1,0:T(8,128)(2,1)}), bf16[4,128,768]{2,1,0:T(8,128)(2,1)S(1)}, u32[]{:S(2)}, u32[]{:S(2)}) %all-to-all-start.2) | async-done | bytes 786464 | tf_op jit(solution)/shard_map/all_to_all | solution.py:294
  189.8 8.0 %all_gather.29 = bf16[512,768]{1,0:T(8,128)(2,1)S(1)} all-gather(bf16[128,768]{1,0:T(8,128)(2,1)S(1)} %add_convert_fusion.3), channel_id=1, replica_groups=mesh['dp'=8,'tensor'=4] {'tensor'}, dimensions={0}, use_global_device_ids=true | all-gather | bytes 983040 | tf_op jit(solution)/shard_map/all_gather | solution.py:382
  201.3 3.5 all-to-all-start.3
  204.9 11.5 %all-to-all-done.3 = bf16[4,128,768]{2,1,0:T(8,128)(2,1)S(1)} async-done(((bf16[4,128,768]{2,1,0:T(8,128)(2,1)}), bf16[4,128,768]{2,1,0:T(8,128)(2,1)S(1)}, u32[]{:S(2)}, u32[]{:S(2)}) %all-to-all-start.3) | async-done | bytes 786464 | tf_op jit(solution)/shard_map/all_to_all | solution.py:294
  217.3 8.4 %all-gather = bf16[544,768]{1,0:T(8,128)(2,1)S(1)} all-gather(bf16[136,768]{1,0:T(8,128)(2,1)S(1)} %pad_maximum_fusion.6), channel_id=2, replica_groups=mesh['dp'=8,'tensor'=4] {'tensor'}, dimensions={0}, use_global_device_ids=true | all-gather | bytes 1044480 | tf_op jit(solution)/shard_map/all_gather | solution.py:393
  228.0 29.4 %shard_map.308 = (bf16[3,512,4096]{2,1,0:T(8,128)(2,1)}, bf16[8,2,192,512]{3,2,1,0:T(8,128)(2,1)}, bf16[192,512]{1,0:T(8,128)(2,1)}) custom-call(s32[8]{0:T(128)} %gather_fusion, s32[8]{0:T(128)} %gather_fusion, s32[128]{0:T(128)} %reshape.258.act_ref, bf16[192,512]{1,0:T(8,128)(2,1)} %fusion.21.q_ref, bf16[8,2,192,512]{3,2,1,0:T(8,128)(2,1)} %copy-done.1, ...), custom_call_target="tpu_custom_call" | custom-call | tf_op jit(solution)/shard_map/pallas_call | solution.py:192
  259.2 7.8 %collective-permute-start.8 = (bf16[2,96,512]{2,1,0:T(8,128)(2,1)}, bf16[2,96,512]{2,1,0:T(8,128)(2,1)}, u32[]{:S(2)}, u32[]{:S(2)}) collective-permute-start(bf16[2,96,512]{2,1,0:T(8,128)(2,1)} %get-tuple-element.167), channel_id=1, source_target_pairs={{0,8},{8,16},{16,24},{24,28},{28,20},{20,12},{12,4},{4,0},{1,9},{9... | collective-permute-start | bytes 589832 | tf_op jit(solution)/shard_map/ppermute | solution.py:276
  267.0 3.2 convolution_convert_fusion
  271.9 12.8 %collective-permute-done.15 = bf16[2,96,512]{2,1,0:T(8,128)(2,1)} collective-permute-done((bf16[2,96,512]{2,1,0:T(8,128)(2,1)}, bf16[2,96,512]{2,1,0:T(8,128)(2,1)}, u32[]{:S(2)}, u32[]{:S(2)}) %collective-permute-start.15) | collective-permute-done | bytes 196640 | tf_op jit(solution)/shard_map/ppermute | solution.py:277
  289.6 5.3 %collective-permute-done.9 = bf16[2,96,512]{2,1,0:T(8,128)(2,1)} collective-permute-done((bf16[2,96,512]{2,1,0:T(8,128)(2,1)}, bf16[2,96,512]{2,1,0:T(8,128)(2,1)}, u32[]{:S(2)}, u32[]{:S(2)}) %collective-permute-start.9) | collective-permute-done | bytes 196640 | tf_op jit(solution)/shard_map/ppermute | solution.py:276
  302.5 3.6 collective-permute-done.10
  312.9 3.3 collective-permute-done.11
  321.1 3.6 collective-permute-done.12
  334.4 3.2 collective-permute-start.14
  337.6 4.4 collective-permute-done.14
  342.0 2.9 collective-permute-done.21
  347.9 3.6 all-to-all-start.4
  354.8 8.4 %all-to-all-done.4 = bf16[4,128,768]{2,1,0:T(8,128)(2,1)S(1)} async-done(((bf16[4,128,768]{2,1,0:T(8,128)(2,1)}), bf16[4,128,768]{2,1,0:T(8,128)(2,1)S(1)}, u32[]{:S(2)}, u32[]{:S(2)}) %all-to-all-start.4) | async-done | bytes 786464 | tf_op jit(solution)/shard_map/all_to_all | solution.py:294
  363.1 3.9 all-to-all-start.5
  369.7 59.6 %reduce-scatter.7.cloned.1.call-done = bf16[96,960]{1,0:T(8,128)(2,1)} async-done(((bf16[768,960]{1,0:T(8,128)(2,1)}), bf16[96,960]{1,0:T(8,128)(2,1)}) %reduce-scatter.7.cloned.1.call-update) | async-done | bytes 184336
  (232 shorter events, 93.8 us)
Async XLA Ops:
  7.2 152.6 %all-gather.5.cloned.1.call-start = ((), (), s32[]{:S(2)}) async-start(), calls=%async_computation.8 | async-start | bytes 1474560 | tf_op jit(solution)/shard_map/all_gather | solution.py:336
  48.2 114.4 %all-gather.7.cloned.1.call-start = ((), (), s32[]{:S(2)}) async-start(), calls=%async_computation.9 | async-start | bytes 1327104 | tf_op jit(solution)/shard_map/all_gather | solution.py:338
  49.6 23.7 %all-to-all-start.1 = ((bf16[8,1,96]{2,1,0:T(2,128)(2,1)}), bf16[8,1,96]{2,1,0:T(2,128)(2,1)S(1)}, u32[]{:S(2)}, u32[]{:S(2)}) async-start(bf16[8,1,96]{2,1,0:T(2,128)(2,1)} %broadcast_in_dim.41), calls=%async_computation.1 | async-start | bytes 8192 | tf_op jit(solution)/shard_map/all_to_all | solution.py:290
  52.9 116.7 %all-gather.9.cloned.1.call-start = ((), (), s32[]{:S(2)}) async-start(), calls=%async_computation.10 | async-start | bytes 1327104 | tf_op jit(solution)/shard_map/all_gather | solution.py:339
  71.1 13.2 %collective-permute-start.1 = (bf16[2,192,512]{2,1,0:T(8,128)(2,1)S(1)}, bf16[2,192,512]{2,1,0:T(8,128)(2,1)}, u32[]{:S(2)}, u32[]{:S(2)}) collective-permute-start(bf16[2,192,512]{2,1,0:T(8,128)(2,1)S(1)} %bitcast.117), channel_id=1, source_target_pairs={{8,0},{16,8},{24,16},{28,24},{20,28},{12,20},{4,12},{0,4},{9,1},{1... | collective-permute-start | bytes 1179656 | tf_op jit(solution)/shard_map/ppermute | solution.py:259
  72.7 13.5 %collective-permute-start = (bf16[2,192,512]{2,1,0:T(8,128)(2,1)S(1)}, bf16[2,192,512]{2,1,0:T(8,128)(2,1)}, u32[]{:S(2)}, u32[]{:S(2)}) collective-permute-start(bf16[2,192,512]{2,1,0:T(8,128)(2,1)S(1)} %bitcast.118), channel_id=1, source_target_pairs={{0,8},{8,16},{16,24},{24,28},{28,20},{20,12},{12,4},{4,0},{1,9},{9... | collective-permute-start | bytes 1179656 | tf_op jit(solution)/shard_map/ppermute | solution.py:258
  84.3 12.6 %collective-permute-start.3 = (bf16[2,192,512]{2,1,0:T(8,128)(2,1)}, bf16[2,192,512]{2,1,0:T(8,128)(2,1)S(1)}, u32[]{:S(2)}, u32[]{:S(2)}) collective-permute-start(bf16[2,192,512]{2,1,0:T(8,128)(2,1)} %collective-permute-done.1), channel_id=1, source_target_pairs={{8,0},{16,8},{24,16},{28,24},{20,28},{12,20},{4,12},{0,4},{9,1},{1... | collective-permute-start | bytes 1179656 | tf_op jit(solution)/shard_map/ppermute | solution.py:259
  86.2 11.4 %collective-permute-start.2 = (bf16[2,192,512]{2,1,0:T(8,128)(2,1)}, bf16[2,192,512]{2,1,0:T(8,128)(2,1)S(1)}, u32[]{:S(2)}, u32[]{:S(2)}) collective-permute-start(bf16[2,192,512]{2,1,0:T(8,128)(2,1)} %collective-permute-done), channel_id=1, source_target_pairs={{0,8},{8,16},{16,24},{24,28},{28,20},{20,12},{12,4},{4,0},{1,9},{9... | collective-permute-start | bytes 1179656 | tf_op jit(solution)/shard_map/ppermute | solution.py:258
  96.9 18.7 %collective-permute-start.5 = (bf16[2,192,512]{2,1,0:T(8,128)(2,1)S(1)}, bf16[2,192,512]{2,1,0:T(8,128)(2,1)S(1)}, u32[]{:S(2)}, u32[]{:S(2)}) collective-permute-start(bf16[2,192,512]{2,1,0:T(8,128)(2,1)S(1)} %collective-permute-done.3), channel_id=1, source_target_pairs={{8,0},{16,8},{24,16},{28,24},{20,28},{12,20},{4,12},{0,4},{9,1},{1... | collective-permute-start | bytes 1179656 | tf_op jit(solution)/shard_map/ppermute | solution.py:259
  97.6 18.1 %collective-permute-start.4 = (bf16[2,192,512]{2,1,0:T(8,128)(2,1)S(1)}, bf16[2,192,512]{2,1,0:T(8,128)(2,1)S(1)}, u32[]{:S(2)}, u32[]{:S(2)}) collective-permute-start(bf16[2,192,512]{2,1,0:T(8,128)(2,1)S(1)} %collective-permute-done.2), channel_id=1, source_target_pairs={{0,8},{8,16},{16,24},{24,28},{28,20},{20,12},{12,4},{4,0},{1,9},{9... | collective-permute-start | bytes 1179656 | tf_op jit(solution)/shard_map/ppermute | solution.py:258
  115.6 6.1 %collective-permute-start.7 = (bf16[2,96,512]{2,1,0:T(8,128)(2,1)S(1)}, bf16[2,96,512]{2,1,0:T(8,128)(2,1)S(1)}, u32[]{:S(2)}, u32[]{:S(2)}) collective-permute-start(bf16[2,96,512]{2,1,0:T(8,128)(2,1)S(1)} %slice.183), channel_id=1, source_target_pairs={{8,0},{16,8},{24,16},{28,24},{20,28},{12,20},{4,12},{0,4},{9,1},{1... | collective-permute-start | bytes 589832 | tf_op jit(solution)/shard_map/ppermute | solution.py:266
  115.7 6.2 %collective-permute-start.6 = (bf16[2,96,512]{2,1,0:T(8,128)(2,1)S(1)}, bf16[2,96,512]{2,1,0:T(8,128)(2,1)S(1)}, u32[]{:S(2)}, u32[]{:S(2)}) collective-permute-start(bf16[2,96,512]{2,1,0:T(8,128)(2,1)S(1)} %slice.182), channel_id=1, source_target_pairs={{0,8},{8,16},{16,24},{24,28},{28,20},{20,12},{12,4},{4,0},{1,9},{9... | collective-permute-start | bytes 589832 | tf_op jit(solution)/shard_map/ppermute | solution.py:265
  172.8 15.1 %all-to-all-start.2 = ((bf16[4,128,768]{2,1,0:T(8,128)(2,1)}), bf16[4,128,768]{2,1,0:T(8,128)(2,1)S(1)}, u32[]{:S(2)}, u32[]{:S(2)}) async-start(bf16[4,128,768]{2,1,0:T(8,128)(2,1)} %bitcast.15), calls=%async_computation.2 | async-start | bytes 1572864 | tf_op jit(solution)/shard_map/all_to_all | solution.py:294
  201.3 15.1 %all-to-all-start.3 = ((bf16[4,128,768]{2,1,0:T(8,128)(2,1)}), bf16[4,128,768]{2,1,0:T(8,128)(2,1)S(1)}, u32[]{:S(2)}, u32[]{:S(2)}) async-start(bf16[4,128,768]{2,1,0:T(8,128)(2,1)} %bitcast.17), calls=%async_computation.3 | async-start | bytes 1572864 | tf_op jit(solution)/shard_map/all_to_all | solution.py:294
  204.8 162.2 %reduce-scatter.5.cloned.1.call-start = ((), (), s32[]{:S(2)}) async-start(), calls=%async_computation.11 | async-start | bytes 1327104 | tf_op jit(solution)/shard_map/reduce_scatter | solution.py:403
  259.2 12.7 %collective-permute-start.8 = (bf16[2,96,512]{2,1,0:T(8,128)(2,1)}, bf16[2,96,512]{2,1,0:T(8,128)(2,1)}, u32[]{:S(2)}, u32[]{:S(2)}) collective-permute-start(bf16[2,96,512]{2,1,0:T(8,128)(2,1)} %get-tuple-element.167), channel_id=1, source_target_pairs={{0,8},{8,16},{16,24},{24,28},{28,20},{20,12},{12,4},{4,0},{1,9},{9... | collective-permute-start | bytes 589832 | tf_op jit(solution)/shard_map/ppermute | solution.py:276
  266.9 17.8 %collective-permute-start.15 = (bf16[2,96,512]{2,1,0:T(8,128)(2,1)}, bf16[2,96,512]{2,1,0:T(8,128)(2,1)}, u32[]{:S(2)}, u32[]{:S(2)}) collective-permute-start(bf16[2,96,512]{2,1,0:T(8,128)(2,1)} %get-tuple-element.168), channel_id=1, source_target_pairs={{8,0},{16,8},{24,16},{28,24},{20,28},{12,20},{4,12},{0,4},{9,1},{1... | collective-permute-start | bytes 589832 | tf_op jit(solution)/shard_map/ppermute | solution.py:277
  270.2 159.1 %reduce-scatter.7.cloned.1.call-start = ((), (), s32[]{:S(2)}) async-start(), calls=%async_computation.12 | async-start | bytes 1769472
  286.8 8.1 %collective-permute-start.9 = (bf16[2,96,512]{2,1,0:T(8,128)(2,1)}, bf16[2,96,512]{2,1,0:T(8,128)(2,1)}, u32[]{:S(2)}, u32[]{:S(2)}) collective-permute-start(bf16[2,96,512]{2,1,0:T(8,128)(2,1)} %get-tuple-element.165), channel_id=1, source_target_pairs={{0,8},{8,16},{16,24},{24,28},{28,20},{20,12},{12,4},{4,0},{1,9},{9... | collective-permute-start | bytes 589832 | tf_op jit(solution)/shard_map/ppermute | solution.py:276
  288.6 7.6 %collective-permute-start.16 = (bf16[2,96,512]{2,1,0:T(8,128)(2,1)}, bf16[2,96,512]{2,1,0:T(8,128)(2,1)}, u32[]{:S(2)}, u32[]{:S(2)}) collective-permute-start(bf16[2,96,512]{2,1,0:T(8,128)(2,1)} %get-tuple-element.166), channel_id=1, source_target_pairs={{8,0},{16,8},{24,16},{28,24},{20,28},{12,20},{4,12},{0,4},{9,1},{1... | collective-permute-start | bytes 589832 | tf_op jit(solution)/shard_map/ppermute | solution.py:277
  297.5 8.5 %collective-permute-start.10 = (bf16[2,96,512]{2,1,0:T(8,128)(2,1)S(1)}, bf16[2,96,512]{2,1,0:T(8,128)(2,1)S(1)}, u32[]{:S(2)}, u32[]{:S(2)}) collective-permute-start(bf16[2,96,512]{2,1,0:T(8,128)(2,1)S(1)} %get-tuple-element.163), channel_id=1, source_target_pairs={{0,8},{8,16},{16,24},{24,28},{28,20},{20,12},{12,4},{4,0},{1,9},{9... | collective-permute-start | bytes 589832 | tf_op jit(solution)/shard_map/ppermute | solution.py:276
  300.3 8.5 %collective-permute-start.17 = (bf16[2,96,512]{2,1,0:T(8,128)(2,1)S(1)}, bf16[2,96,512]{2,1,0:T(8,128)(2,1)S(1)}, u32[]{:S(2)}, u32[]{:S(2)}) collective-permute-start(bf16[2,96,512]{2,1,0:T(8,128)(2,1)S(1)} %get-tuple-element.164), channel_id=1, source_target_pairs={{8,0},{16,8},{24,16},{28,24},{20,28},{12,20},{4,12},{0,4},{9,1},{1... | collective-permute-start | bytes 589832 | tf_op jit(solution)/shard_map/ppermute | solution.py:277
  310.0 6.1 %collective-permute-start.11 = (bf16[2,96,512]{2,1,0:T(8,128)(2,1)S(1)}, bf16[2,96,512]{2,1,0:T(8,128)(2,1)S(1)}, u32[]{:S(2)}, u32[]{:S(2)}) collective-permute-start(bf16[2,96,512]{2,1,0:T(8,128)(2,1)S(1)} %get-tuple-element.161), channel_id=1, source_target_pairs={{0,8},{8,16},{16,24},{24,28},{28,20},{20,12},{12,4},{4,0},{1,9},{9... | collective-permute-start | bytes 589832 | tf_op jit(solution)/shard_map/ppermute | solution.py:276
  311.9 5.7 %collective-permute-start.18 = (bf16[2,96,512]{2,1,0:T(8,128)(2,1)S(1)}, bf16[2,96,512]{2,1,0:T(8,128)(2,1)S(1)}, u32[]{:S(2)}, u32[]{:S(2)}) collective-permute-start(bf16[2,96,512]{2,1,0:T(8,128)(2,1)S(1)} %get-tuple-element.162), channel_id=1, source_target_pairs={{8,0},{16,8},{24,16},{28,24},{20,28},{12,20},{4,12},{0,4},{9,1},{1... | collective-permute-start | bytes 589832 | tf_op jit(solution)/shard_map/ppermute | solution.py:277
  318.7 6.0 %collective-permute-start.12 = (bf16[2,96,512]{2,1,0:T(8,128)(2,1)S(1)}, bf16[2,96,512]{2,1,0:T(8,128)(2,1)S(1)}, u32[]{:S(2)}, u32[]{:S(2)}) collective-permute-start(bf16[2,96,512]{2,1,0:T(8,128)(2,1)S(1)} %get-tuple-element.159), channel_id=1, source_target_pairs={{0,8},{8,16},{16,24},{24,28},{28,20},{20,12},{12,4},{4,0},{1,9},{9... | collective-permute-start | bytes 589832 | tf_op jit(solution)/shard_map/ppermute | solution.py:276
  319.8 5.7 %collective-permute-start.19 = (bf16[2,96,512]{2,1,0:T(8,128)(2,1)S(1)}, bf16[2,96,512]{2,1,0:T(8,128)(2,1)S(1)}, u32[]{:S(2)}, u32[]{:S(2)}) collective-permute-start(bf16[2,96,512]{2,1,0:T(8,128)(2,1)S(1)} %get-tuple-element.160), channel_id=1, source_target_pairs={{8,0},{16,8},{24,16},{28,24},{20,28},{12,20},{4,12},{0,4},{9,1},{1... | collective-permute-start | bytes 589832 | tf_op jit(solution)/shard_map/ppermute | solution.py:277
  326.6 6.3 %collective-permute-start.13 = (bf16[2,96,512]{2,1,0:T(8,128)(2,1)S(1)}, bf16[2,96,512]{2,1,0:T(8,128)(2,1)S(1)}, u32[]{:S(2)}, u32[]{:S(2)}) collective-permute-start(bf16[2,96,512]{2,1,0:T(8,128)(2,1)S(1)} %get-tuple-element.157), channel_id=1, source_target_pairs={{0,8},{8,16},{16,24},{24,28},{28,20},{20,12},{12,4},{4,0},{1,9},{9... | collective-permute-start | bytes 589832 | tf_op jit(solution)/shard_map/ppermute | solution.py:276
  327.2 6.1 %collective-permute-start.20 = (bf16[2,96,512]{2,1,0:T(8,128)(2,1)S(1)}, bf16[2,96,512]{2,1,0:T(8,128)(2,1)S(1)}, u32[]{:S(2)}, u32[]{:S(2)}) collective-permute-start(bf16[2,96,512]{2,1,0:T(8,128)(2,1)S(1)} %get-tuple-element.158), channel_id=1, source_target_pairs={{8,0},{16,8},{24,16},{28,24},{20,28},{12,20},{4,12},{0,4},{9,1},{1... | collective-permute-start | bytes 589832 | tf_op jit(solution)/shard_map/ppermute | solution.py:277
  334.4 7.7 %collective-permute-start.14 = (bf16[2,96,512]{2,1,0:T(8,128)(2,1)S(1)}, bf16[2,96,512]{2,1,0:T(8,128)(2,1)S(1)}, u32[]{:S(2)}, u32[]{:S(2)}) collective-permute-start(bf16[2,96,512]{2,1,0:T(8,128)(2,1)S(1)} %get-tuple-element.155), channel_id=1, source_target_pairs={{0,8},{8,16},{16,24},{24,28},{28,20},{20,12},{12,4},{4,0},{1,9},{9... | collective-permute-start | bytes 589832 | tf_op jit(solution)/shard_map/ppermute | solution.py:276
  337.6 7.3 %collective-permute-start.21 = (bf16[2,96,512]{2,1,0:T(8,128)(2,1)S(1)}, bf16[2,96,512]{2,1,0:T(8,128)(2,1)S(1)}, u32[]{:S(2)}, u32[]{:S(2)}) collective-permute-start(bf16[2,96,512]{2,1,0:T(8,128)(2,1)S(1)} %get-tuple-element.156), channel_id=1, source_target_pairs={{8,0},{16,8},{24,16},{28,24},{20,28},{12,20},{4,12},{0,4},{9,1},{1... | collective-permute-start | bytes 589832 | tf_op jit(solution)/shard_map/ppermute | solution.py:277
  347.9 15.3 %all-to-all-start.4 = ((bf16[4,128,768]{2,1,0:T(8,128)(2,1)}), bf16[4,128,768]{2,1,0:T(8,128)(2,1)S(1)}, u32[]{:S(2)}, u32[]{:S(2)}) async-start(bf16[4,128,768]{2,1,0:T(8,128)(2,1)} %bitcast.38), calls=%async_computation.4 | async-start | bytes 1572864 | tf_op jit(solution)/shard_map/all_to_all | solution.py:294
  363.1 68.9 %all-to-all-start.5 = ((bf16[8,128,576]{1,2,0:T(8,128)(2,1)}), bf16[8,128,576]{1,2,0:T(8,128)(2,1)S(1)}, u32[]{:S(2)}, u32[]{:S(2)}) async-start(bf16[8,128,576]{1,2,0:T(8,128)(2,1)} %copy.101), calls=%async_computation.5 | async-start | bytes 2359296 | tf_op jit(solution)/shard_map/all_to_all | solution.py:432
  (35 other events, 300.6 us)
Sparse Core Ops, SparseCore 0:
  48.3 18.7 all-gather.4
  69.3 47.3 all-gather.6
  118.8 41.9 all-gather.8
  270.3 78.9 reduce-scatter.4
  352.6 76.6 reduce-scatter.6
